TPU v7x, 32 devices: a whole 2x2x4 slice. The times are simulated.
32 devices in a mesh: wide: 16 (over z, y, x), clus: 2 (over core).
Axes of the slice: x: 2, y: 2, z: 4, core: 2. Of those that a mesh axis runs over, the one named last changes fastest.
Arguments:
- duals: bfloat16 [96, 64, 3840], P(None, ('wide', 'clus')), may hold values from -6 to 6
- kernel: bfloat16 [64, 6, 3840], P(('wide', 'clus')), may hold values from -0.29882812 to 0.29882812
- sub_counts: int32 [32], P(('wide', 'clus')), may hold values from 1 to 2, as said below
- dual_sizes: int32 [64], P(('wide', 'clus')), may hold values from 1920 to 3840, as said below
- cluster_factor: float32 [16, 24, 24], P('wide'), as said below
- coarse_map: int32 [16, 24], P('wide'), may hold values from 0 to 383, as said below
- coarse_inverse: float32 [384, 384], P(None, 'clus'), as said below
Outputs:
- projected: bfloat16 [96, 64, 3840], P(None, ('wide', 'clus'))
Inputs may be any that keep to these rules, and one draw needn't show every extreme that they name: `sub_counts`: each device holds 1 to 2 subdomains; some device holds 2. `dual_sizes`: some slot has the full 3840. `coarse_map`: the rows of cluster w map into the 48 global rows that begin at w * 24, counted modulo 384. `cluster_factor`: lower triangular with diagonal entries between 1 and 2. `coarse_inverse`: diagonal entries between 1 and 2.
All inputs are finite; a program needn't handle non-finite values.
Results may differ from a plain program's by a relative error of at most 0.0018.
Values sent between devices are 32-bit elements; how exact they have to be, the bound alone decides.
No kernel may reach another device: no remote copies, remote signals or barrier semaphores. Data moves between devices by JAX's collectives and lax.ppermute only.
A program may use at most 64 MiB of HBM per device.

v0:
```python
import jax
import jax.numpy as jnp
from jax import lax
from jax.sharding import PartitionSpec as P


def per_device(duals, kernel, sub_counts, dual_sizes, cluster_factor, coarse_map, coarse_inverse):
    rhs_count, sub_count, dual_width = duals.shape
    mode_count = kernel.shape[1]
    hi = lax.Precision.HIGHEST
    position = lax.broadcasted_iota(jnp.int32, (sub_count, dual_width), 1)
    slot_index = lax.broadcasted_iota(jnp.int32, (sub_count, dual_width), 0)
    active = (position < dual_sizes[:, None]) & (slot_index < sub_counts[0])
    masked = jnp.where(active[:, None, :], kernel, jnp.zeros_like(kernel))
    local = jnp.einsum("rsi,ski->rsk", duals, masked, preferred_element_type=jnp.float32)
    local = local.reshape(rhs_count, sub_count * mode_count)
    cluster_vec = lax.all_gather(local, "clus", axis=1, tiled=True)
    lower = cluster_factor[0]
    rows_map = coarse_map[0]
    cluster_rows = rows_map.shape[0]
    global_rows = coarse_inverse.shape[0]
    forward = lax.linalg.triangular_solve(lower, cluster_vec.T, left_side=True, lower=True).T
    one_hot = (
        rows_map[:, None] == lax.broadcasted_iota(jnp.int32, (cluster_rows, global_rows), 1)
    ).astype(jnp.float32)
    part_sum = jnp.dot(forward, one_hot, precision=hi)
    gsum = lax.psum(part_sum, "wide")
    beta_part = jnp.dot(gsum, coarse_inverse, precision=hi)
    beta = lax.all_gather(beta_part, "clus", axis=1, tiled=True)
    back = jnp.dot(beta, one_hot.T, precision=hi)
    corr = lax.linalg.triangular_solve(
        lower, (forward - back).T, left_side=True, lower=True, transpose_a=True
    )
    own_rows = lax.dynamic_slice_in_dim(
        corr, lax.axis_index("clus") * sub_count * mode_count, sub_count * mode_count, 0
    )
    own_corr = own_rows.T.reshape(rhs_count, sub_count, mode_count).astype(jnp.bfloat16)
    delta = jnp.einsum("rsk,ski->rsi", own_corr, masked, preferred_element_type=jnp.float32)
    return (duals.astype(jnp.float32) - delta).astype(jnp.bfloat16)


def solution(mesh):
    in_specs = (
        P(None, ("wide", "clus"), None),
        P(("wide", "clus"), None, None),
        P(("wide", "clus")),
        P(("wide", "clus")),
        P("wide", None, None),
        P("wide", None),
        P(None, "clus"),
    )
    out_specs = P(None, ("wide", "clus"), None)
    return jax.shard_map(
        per_device, mesh=mesh, in_specs=in_specs, out_specs=out_specs, check_vma=False
    )
```

profile of v0, /device:TPU:0, one launch (start us, length us, event | category | flops | bytes accessed | tf_op | source)
XLA Modules:
  0.0 140.0 jit_solution(6165059862386261918)
XLA Ops:
  6.5 0.0 copy-start
  6.5 0.0 copy-start.2
  6.5 0.0 all-reduce.2.cloned.1.call-start
  7.3 0.7 fusion.16
  8.0 1.8 %custom-call.5 = f32[1,24,24]{1,2,0:T(8,128)S(1)} custom-call(f32[1,24,24]{2,1,0:T(8,128)S(1)} %fusion.16), custom_call_target="InvertDiagBlocksLowerTriangular" | custom-call | tf_op jit(solution)/shard_map/triangular_solve | solution.py:31
  9.8 0.8 compare_and_fusion
  10.6 1.0 broadcast_select_fusion
  11.6 0.0 copy-start.1
  11.6 2.0 %fusion.4 = f32[96,2,6]{0,2,1:T(8,128)S(1)} fusion(bf16[96,2,3840]{2,1,0:T(2,128)(2,1)} %param.7, bf16[2,6,3840]{2,0,1:T(2,128)(2,1)S(1)} %broadcast_select_fusion), kind=kOutput, calls=%fused_computation.6 | convolution fusion | flops 8847360 | bytes 1571328 | tf_op jit(solution)/shard_map/rsi,ski->rsk/dot_general | solution.py:15
  13.5 2.0 %all-gather = f32[2,12,96]{2,1,0:T(8,128)S(1)} all-gather(f32[1,12,96]{2,1,0:T(8,128)S(1)} %bitcast.34), channel_id=1, replica_groups=mesh['wide'=16,'clus'=2] {'clus'}, dimensions={0}, use_global_device_ids=true | all-gather | bytes 13824 | tf_op jit(solution)/shard_map/all_gather | solution.py:17
  15.5 0.2 fusion.14
  15.7 0.0 copy-done.2
  15.7 0.9 fusion.9
  16.7 0.0 all-reduce.2.cloned.1.call-update
  16.7 109.5 %all-reduce.2.cloned.1.call-done = f32[96,384]{1,0:T(8,128)} async-done(((f32[96,384]{1,0:T(8,128)}), f32[96,384]{1,0:T(8,128)}) %all-reduce.2.cloned.1.call-update) | async-done | bytes 147472 | tf_op jit(solution)/shard_map/psum | solution.py:27
  126.2 0.0 copy-done
  126.2 1.3 fusion.18
  127.5 1.9 %all_gather.7 = f32[96,384]{0,1:T(8,128)S(1)} all-gather(f32[96,192]{0,1:T(8,128)S(1)} %fusion.18), channel_id=1, replica_groups=mesh['wide'=16,'clus'=2] {'clus'}, dimensions={1}, use_global_device_ids=true | all-gather | bytes 221184 | tf_op jit(solution)/shard_map/all_gather | solution.py:29
  129.5 0.2 convolution_subtract_fusion
  129.7 0.1 fusion.12
  129.9 0.0 copy-done.1
  129.9 0.6 fusion.1
  130.5 2.6 %copy.23 = bf16[96,2,3840]{2,1,0:T(2,128)(2,1)} copy(bf16[96,2,3840]{2,0,1:T(8,128)(2,1)S(1)} %fusion.1) | data formatting | bytes 2949120 | tf_op jit(solution)/shard_map/convert_element_type | solution.py:39
  (5 shorter events, 0.1 us)
Async XLA Ops:
  6.5 119.7 %copy-start = (f32[384,192]{0,1:T(8,128)S(1)}, f32[384,192]{0,1:T(8,128)}, u32[]{:S(2)}) copy-start(f32[384,192]{0,1:T(8,128)} %param.13) | copy-start | bytes 884740
  6.5 9.2 %copy-start.2 = (s32[1,24]{1,0:T(1,128)S(1)}, s32[1,24]{1,0:T(1,128)}, u32[]{:S(2)}) copy-start(s32[1,24]{1,0:T(1,128)} %param.12) | copy-start | bytes 292
  6.5 119.7 %all-reduce.2.cloned.1.call-start = ((), (), s32[]{:S(2)}) async-start(), calls=%async_computation | async-start | bytes 294912 | tf_op jit(solution)/shard_map/psum | solution.py:27
  11.6 118.3 %copy-start.1 = (bf16[96,2,3840]{2,1,0:T(2,128)(2,1)S(1)}, bf16[96,2,3840]{2,1,0:T(2,128)(2,1)}, u32[]{:S(2)}) copy-start(bf16[96,2,3840]{2,1,0:T(2,128)(2,1)} %param.7) | copy-start | bytes 4423684
Sparse Core Ops, SparseCore 0:
  16.8 109.3 all-reduce.1
where the time goes:
time: 140 us
  waiting for transfers between devices  110 us (79%)
  between operations  14.2 us (10%)
  matrix products  5.34 us (4%)
  other arithmetic  4.31 us (3%)
  blocking collectives  3.92 us (3%)
  local copies, waits for them, and re-layouts  2.7 us (2%)
    psum x1, waiting for transfers between devices, per_device(): gsum = lax.psum(part_sum, 'wide')  110 us
  transfers between devices with their start and end apart: 1, of which 1 were waited for; matrix products, arithmetic and copies ran while one was open for 0% of the time, Pallas kernels for 0%

commit v1 on v0

--- a/solution.py
+++ b/solution.py
@@ -24,7 +24,7 @@
         rows_map[:, None] == lax.broadcasted_iota(jnp.int32, (cluster_rows, global_rows), 1)
     ).astype(jnp.float32)
     part_sum = jnp.dot(forward, one_hot, precision=hi)
-    gsum = lax.psum(part_sum, "wide")
+    gsum = jnp.sum(lax.all_gather(part_sum, "wide"), axis=0)
     beta_part = jnp.dot(gsum, coarse_inverse, precision=hi)
     beta = lax.all_gather(beta_part, "clus", axis=1, tiled=True)
     back = jnp.dot(beta, one_hot.T, precision=hi)

time: 140 us -> 96.5 us (0.69)
  waiting for transfers between devices: 110 us -> 64.9 us
  other arithmetic: 4.31 us -> 6.21 us
    psum x1 -> x0, waiting for transfers between devices: 110 us -> none  [per_device(): gsum = lax.psum(part_sum, 'wide')]
    all_gather x0 -> x1, waiting for transfers between devices: none -> 64.9 us  [per_device(): gsum = jnp.sum(lax.all_gather(part_sum, 'wide'), axis=0)]
    reduce_sum x0 -> x1, other arithmetic: none -> 1.91 us  [per_device(): gsum = jnp.sum(lax.all_gather(part_sum, 'wide'), axis=0)]
where the time goes in v1:
time: 96.5 us; the launch traced here: 96.3 us
  waiting for transfers between devices  64.9 us (67%)
  between operations  14.2 us (15%)
  other arithmetic  6.21 us (6%)
  matrix products  4.32 us (4%)
  blocking collectives  3.92 us (4%)
  local copies, waits for them, and re-layouts  2.69 us (3%)
    all_gather x1, waiting for transfers between devices, per_device(): gsum = jnp.sum(lax.all_gather(part_sum, 'wide'), axis=0)  64.9 us
    convert_element_type x1, local copies, waits for them, and re-layouts, per_device(): return (duals.astype(jnp.float32) - delta).astype(jnp.bfloat16)  2.63 us
    another operation x2, other arithmetic, per_device(): lax.linalg.triangular_solve(lower, (forward - back).T, left_side=True, lo...  2.55 us
    all_gather x1, blocking collectives, per_device(): cluster_vec = lax.all_gather(local, 'clus', axis=1, tiled=True)  1.97 us
    all_gather x1, blocking collectives, per_device(): beta = lax.all_gather(beta_part, 'clus', axis=1, tiled=True)  1.95 us
  transfers between devices with their start and end apart: 1, of which 1 were waited for; matrix products, arithmetic and copies ran while one was open for 0% of the time, Pallas kernels for 0%

profile of v1, /device:TPU:0, one launch (start us, length us, event | category | flops | bytes accessed | tf_op | source)
XLA Modules:
  0.0 96.3 jit_solution(3194218232913824929)
XLA Ops:
  6.5 0.0 copy-start
  6.5 0.0 copy-start.2
  6.5 0.0 all-gather.4.cloned.1.call-start
  7.3 0.7 fusion.16
  8.0 1.8 %custom-call.5 = f32[1,24,24]{1,2,0:T(8,128)S(1)} custom-call(f32[1,24,24]{2,1,0:T(8,128)S(1)} %fusion.16), custom_call_target="InvertDiagBlocksLowerTriangular" | custom-call | tf_op jit(solution)/shard_map/triangular_solve | solution.py:31
  9.8 0.8 compare_and_fusion
  10.6 1.0 %broadcast_select_fusion = bf16[2,6,3840]{2,0,1:T(2,128)(2,1)S(1)} fusion(bf16[2,6,3840]{2,0,1:T(2,128)(2,1)} %param.8, pred[2,3840]{1,0:T(4,128)(4,1)S(1)} %compare_and_fusion), kind=kLoop, calls=%fused_computation.7 | loop fusion | flops 46080 | bytes 192000 | tf_op jit(solution)/shard_map/jit(_where)/select_n | solution.py:14
  11.6 1.9 %fusion.4 = f32[96,2,6]{0,2,1:T(8,128)S(1)} fusion(bf16[96,2,3840]{2,1,0:T(2,128)(2,1)} %param.7, bf16[2,6,3840]{2,0,1:T(2,128)(2,1)S(1)} %broadcast_select_fusion), kind=kOutput, calls=%fused_computation.6 | convolution fusion | flops 8847360 | bytes 1571328 | tf_op jit(solution)/shard_map/rsi,ski->rsk/dot_general | solution.py:15
  13.4 2.0 %all-gather.1 = f32[2,12,96]{2,1,0:T(8,128)S(1)} all-gather(f32[1,12,96]{2,1,0:T(8,128)S(1)} %bitcast.36), channel_id=1, replica_groups=mesh['wide'=16,'clus'=2] {'clus'}, dimensions={0}, use_global_device_ids=true | all-gather | bytes 13824 | tf_op jit(solution)/shard_map/all_gather | solution.py:17
  15.4 0.2 fusion.14
  15.6 0.0 copy-done.2
  15.6 0.9 fusion.9
  16.5 0.0 all-gather.4.cloned.1.call-update
  16.6 64.9 %all-gather.4.cloned.1.call-done = f32[1536,384]{1,0:T(8,128)} async-done(((f32[96,384]{1,0:T(8,128)}), f32[1536,384]{1,0:T(8,128)}) %all-gather.4.cloned.1.call-update) | async-done | bytes 2359312 | tf_op jit(solution)/shard_map/all_gather | solution.py:27
  81.5 0.0 copy-start.1
  81.5 1.9 %reduce_sum.9 = f32[96,384]{1,0:T(8,128)S(1)} reduce(f32[16,96,384]{2,1,0:T(8,128)} %bitcast.35, f32[]{:T(128)} %constant.19.clone.1), dimensions={0}, to_apply=%region_0.1 | reduce | flops 552960 | bytes 2506756 | tf_op jit(solution)/shard_map/reduce_sum | solution.py:27
  83.4 0.0 copy-done
  83.4 0.4 fusion.18
  83.8 1.9 %all_gather.15 = f32[96,384]{0,1:T(8,128)S(1)} all-gather(f32[96,192]{0,1:T(8,128)S(1)} %fusion.18), channel_id=1, replica_groups=mesh['wide'=16,'clus'=2] {'clus'}, dimensions={1}, use_global_device_ids=true | all-gather | bytes 221184 | tf_op jit(solution)/shard_map/all_gather | solution.py:29
  85.8 0.2 convolution_subtract_fusion
  86.0 0.1 fusion.12
  86.2 0.0 copy-done.1
  86.2 0.6 fusion.1
  86.8 2.6 %copy.23 = bf16[96,2,3840]{2,1,0:T(2,128)(2,1)} copy(bf16[96,2,3840]{2,0,1:T(8,128)(2,1)S(1)} %fusion.1) | data formatting | bytes 2949120 | tf_op jit(solution)/shard_map/convert_element_type | solution.py:39
  (5 shorter events, 0.1 us)
Async XLA Ops:
  6.5 76.9 %copy-start = (f32[384,192]{0,1:T(8,128)S(1)}, f32[384,192]{0,1:T(8,128)}, u32[]{:S(2)}) copy-start(f32[384,192]{0,1:T(8,128)} %param.13) | copy-start | bytes 884740
  6.5 9.1 %copy-start.2 = (s32[1,24]{1,0:T(1,128)S(1)}, s32[1,24]{1,0:T(1,128)}, u32[]{:S(2)}) copy-start(s32[1,24]{1,0:T(1,128)} %param.12) | copy-start | bytes 292
  6.5 75.0 %all-gather.4.cloned.1.call-start = ((), (), s32[]{:S(2)}) async-start(), calls=%async_computation | async-start | bytes 2506752 | tf_op jit(solution)/shard_map/all_gather | solution.py:27
  81.5 4.7 %copy-start.1 = (bf16[96,2,3840]{2,1,0:T(2,128)(2,1)S(1)}, bf16[96,2,3840]{2,1,0:T(2,128)(2,1)}, u32[]{:S(2)}) copy-start(bf16[96,2,3840]{2,1,0:T(2,128)(2,1)} %param.7) | copy-start | bytes 4423684
Sparse Core Ops, SparseCore 0:
  16.7 64.7 all-gather.3
